TPU v7x, 32 devices: a whole 2x2x4 slice. The times are simulated.
32 devices in a mesh: dp: 4 (over y, x), filter: 8 (over z, core).
Axes of the slice: x: 2, y: 2, z: 4, core: 2. Of those that a mesh axis runs over, the one named last changes fastest.
Arguments:
- fields: bfloat16 [4, 32, 32, 1024], P('dp', None, None, 'filter'), may hold values from -6 to 6
- weight_one: bfloat16 [3, 3, 1024, 1024], P(None, None, 'dp', 'filter'), may hold values from -0.0625 to 0.0625
- weight_two: bfloat16 [3, 3, 1024, 1024], P(None, None, 'dp', 'filter'), may hold values from -0.0625 to 0.0625
- cotangent: bfloat16 [4, 32, 32, 1024], P('dp', None, None, 'filter'), may hold values from -6 to 6
Outputs:
- output: bfloat16 [4, 32, 32, 1024], P('dp', None, None, 'filter')
- grad_one: float32 [3, 3, 1024, 1024], P(None, None, 'dp', 'filter')
- grad_two: float32 [3, 3, 1024, 1024], P(None, None, 'dp', 'filter')
All inputs are finite; a program needn't handle non-finite values.
Results may differ from a plain program's by a relative error of at most 0.018.
Values may be sent and summed in bfloat16 or wider, within the bound.
No kernel may reach another device: no remote copies, remote signals or barrier semaphores. Data moves between devices by JAX's collectives and lax.ppermute only.
A program may use at most 128 MiB of HBM per device.

v0:
```python
import jax
import jax.numpy as jnp
from jax import lax
from jax.sharding import PartitionSpec as P


def shift_cells(values, row_step, col_step):
    size = values.shape[1]
    padded = jnp.pad(values, ((0, 0), (1, 1), (1, 1), (0, 0)))
    return padded[:, 1 + row_step : 1 + row_step + size, 1 + col_step : 1 + col_step + size, :]


def conv_taps(inputs, weights):
    products = jnp.einsum("bhwc,pqcd->bhwpqd", inputs, weights, preferred_element_type=jnp.float32)
    result = jnp.zeros(inputs.shape[:3] + (weights.shape[3],), jnp.float32)
    for row_tap in range(3):
        for col_tap in range(3):
            result = result + shift_cells(
                products[:, :, :, row_tap, col_tap, :], row_tap - 1, col_tap - 1
            )
    return result


def shifted_stack(grads):
    pieces = []
    for row_tap in range(3):
        for col_tap in range(3):
            pieces.append(shift_cells(grads, 1 - row_tap, 1 - col_tap))
    return jnp.stack(pieces, axis=3).reshape(grads.shape[:3] + (3, 3, grads.shape[3]))


def transposed(grads, weights):
    stacked = shifted_stack(grads)
    return jnp.einsum("bhwpqd,pqcd->bhwc", stacked, weights, preferred_element_type=jnp.float32)


def filter_grads(inputs, grads):
    stacked = shifted_stack(grads)
    return jnp.einsum("bhwc,bhwpqd->pqcd", inputs, stacked, preferred_element_type=jnp.float32)


def body(fields, weight_one, weight_two, cotangent):
    full_one = lax.all_gather(weight_one, "dp", axis=2, tiled=True)
    gathered = lax.all_gather(fields, "filter", axis=3, tiled=True)
    pre_one = conv_taps(gathered, full_one)
    hidden = jax.nn.silu(pre_one).astype(jnp.bfloat16)
    hidden_all = lax.all_gather(hidden, "filter", axis=3, tiled=True)
    full_two = lax.all_gather(weight_two, "dp", axis=2, tiled=True)
    output = conv_taps(hidden_all, full_two).astype(jnp.bfloat16)
    grad_two = lax.psum_scatter(
        filter_grads(hidden_all, cotangent).astype(jnp.bfloat16),
        "dp",
        scatter_dimension=2,
        tiled=True,
    ).astype(jnp.float32)
    partial_back = transposed(cotangent, full_two)
    back = lax.psum_scatter(
        partial_back.astype(jnp.bfloat16), "filter", scatter_dimension=3, tiled=True
    ).astype(jnp.float32)
    sigma = jax.nn.sigmoid(pre_one)
    back_pre = (back * sigma * (1.0 + pre_one * (1.0 - sigma))).astype(jnp.bfloat16)
    grad_one = lax.psum_scatter(
        filter_grads(gathered, back_pre).astype(jnp.bfloat16), "dp", scatter_dimension=2, tiled=True
    ).astype(jnp.float32)
    return (output, grad_one, grad_two)


def solution(mesh):
    placed = (
        P("dp", None, None, "filter"),
        P(None, None, "dp", "filter"),
        P(None, None, "dp", "filter"),
        P("dp", None, None, "filter"),
    )
    return jax.shard_map(
        body,
        mesh=mesh,
        in_specs=placed,
        out_specs=(
            P("dp", None, None, "filter"),
            P(None, None, "dp", "filter"),
            P(None, None, "dp", "filter"),
        ),
        check_vma=False,
    )
```

profile of v0, /device:TPU:0, one launch (start us, length us, event | category | flops | bytes accessed | tf_op | source)
XLA Modules:
  0.0 284.4 jit_solution(1730159838617975054)
XLA Ops:
  7.2 0.7 all-gather.11.cloned.1.call-update
  8.0 0.7 all-gather.7.cloned.1.call-update
  8.7 0.0 all-gather.5.cloned.1.call-start
  8.7 0.7 all-gather.5.cloned.1.call-update
  9.4 0.0 reduce-scatter.10.cloned.1.call-start
  9.4 1.0 fusion.41
  10.5 1.0 fusion.43
  11.5 0.1 fusion.45
  11.6 0.1 fusion.47
  11.7 0.1 fusion.49
  11.8 0.1 fusion.51
  12.0 0.1 fusion.55
  12.1 38.0 %all-gather.11.cloned.1.call-done = bf16[3,3,1024,128]{3,2,1,0:T(8,128)(2,1)} async-done(((bf16[3,3,256,128]{3,2,1,0:T(8,128)(2,1)}), bf16[3,3,1024,128]{3,2,1,0:T(8,128)(2,1)}) %all-gather.11.cloned.1.call-update) | async-done | bytes 2359312 | tf_op jit(solution)/shard_map/all_gather | solution.py:48
  50.1 5.3 %fusion.16 = bf16[1,32,32,1024]{3,2,1,0:T(8,128)(2,1)S(1)} fusion(bf16[32,32,3,3,128]{4,1,0,3,2:T(8,128)(2,1)} %bitcast.223, bf16[3,3,1024,128]{3,2,1,0:T(8,128)(2,1)} %all-gather.11.cloned.1.call-done), kind=kOutput, calls=%fused_computation.15 | convolution fusion | flops 2416967680 | bytes 6815744 | tf_op jit(solution)/shard_map/bhwpqd,pqcd->bhwc/dot_general | solution.py:34
  55.4 12.2 %copy.60 = bf16[1,32,32,1024]{2,1,0,3:T(8,128)(2,1)} copy(bf16[1,32,32,1024]{3,2,1,0:T(8,128)(2,1)S(1)} %fusion.16) | data formatting | bytes 4194304
  67.5 12.5 %reshape.42 = bf16[1024,1024]{1,0:T(8,128)(2,1)} reshape(bf16[1024,1,32,32]{3,2,1,0:T(8,128)(2,1)} %bitcast.220) | data formatting | bytes 4194304
  80.0 0.0 all-gather.9.cloned.1.call-start
  80.0 9.4 %all-gather.7.cloned.1.call-done = bf16[3,3,1024,128]{3,2,1,0:T(8,128)(2,1)} async-done(((bf16[3,3,256,128]{3,2,1,0:T(8,128)(2,1)}), bf16[3,3,1024,128]{3,2,1,0:T(8,128)(2,1)}) %all-gather.7.cloned.1.call-update) | async-done | bytes 2359312 | tf_op jit(solution)/shard_map/all_gather | solution.py:43
  89.4 32.5 %all-gather.5.cloned.1.call-done = bf16[1,32,32,1024]{3,2,1,0:T(8,128)(2,1)} async-done(((bf16[1,32,32,128]{3,2,1,0:T(8,128)(2,1)}), bf16[1,32,32,1024]{3,2,1,0:T(8,128)(2,1)}) %all-gather.5.cloned.1.call-update) | async-done | bytes 2097168 | tf_op jit(solution)/shard_map/all_gather | solution.py:44
  121.9 5.2 %fusion.10 = f32[1,32,32,3,3,128]{5,2,4,3,1,0:T(8,128)S(1)} fusion(bf16[3,3,1024,128]{3,2,1,0:T(8,128)(2,1)} %all-gather.7.cloned.1.call-done, bf16[1,32,32,1024]{3,2,1,0:T(8,128)(2,1)} %all-gather.5.cloned.1.call-done), kind=kOutput, calls=%fused_computation.13 | convolution fusion | flops 2415919104 | bytes 9175040 | tf_op jit(solution)/shard_map/bhwc,pqcd->bhwpqd/dot_general | solution.py:14
  127.1 2.1 copy-done.1
  129.2 1.8 slice_bitcast_fusion.17
  130.9 28.0 %reduce-scatter.10.cloned.1.call-done = bf16[128,1024]{1,0:T(8,128)(2,1)} async-done(((bf16[1024,1024]{1,0:T(8,128)(2,1)}), bf16[128,1024]{1,0:T(8,128)(2,1)}) %reduce-scatter.10.cloned.1.call-update) | async-done | bytes 262160
  158.9 1.8 reshape.43
  160.7 1.8 copy.61
  162.5 2.3 multiply_convert_fusion
  164.8 0.8 multiply_convert_fusion.1
  165.7 0.2 reduce-scatter.6.cloned.1.call-start
  165.9 0.1 fusion.57
  166.0 0.1 fusion.61
  166.1 0.1 fusion.63
  166.3 0.1 fusion.65
  166.4 0.1 fusion.67
  166.5 0.1 fusion.71
  166.6 0.9 copy-done.5
  167.5 4.0 %fusion = bf16[3,3,1024,128]{2,3,1,0:T(8,128)(2,1)} fusion(bf16[32,32,3,3,128]{4,1,0,3,2:T(8,128)(2,1)S(1)} %bitcast.225, bf16[1,32,32,1024]{3,2,1,0:T(8,128)(2,1)S(1)} %copy-done.5), kind=kOutput, calls=%fused_computation.3 | convolution fusion | flops 2417098752 | bytes 6815744 | tf_op jit(solution)/shard_map/bhwc,bhwpqd->pqcd/dot_general | solution.py:39
  171.5 0.0 reduce-scatter.8.cloned.1.call-start
  171.6 23.8 %all-gather.9.cloned.1.call-done = bf16[1,32,32,1024]{3,2,1,0:T(8,128)(2,1)} async-done(((bf16[1,32,32,128]{3,2,1,0:T(8,128)(2,1)}), bf16[1,32,32,1024]{3,2,1,0:T(8,128)(2,1)}) %all-gather.9.cloned.1.call-update) | async-done | bytes 2097168 | tf_op jit(solution)/shard_map/all_gather | solution.py:47
  195.4 4.2 %fusion.4 = bf16[3,3,128,1024,1]{3,2,0,1,4:T(8,128)(2,1)S(1)} fusion(bf16[32,32,3,3,128]{4,1,0,3,2:T(8,128)(2,1)S(1)} %bitcast.224, bf16[1,32,32,1024]{3,2,1,0:T(8,128)(2,1)} %all-gather.9.cloned.1.call-done), kind=kOutput, calls=%fused_computation.7 | convolution fusion | flops 2415919104 | bytes 6815744 | tf_op jit(solution)/shard_map/bhwc,bhwpqd->pqcd/dot_general | solution.py:39
  199.6 1.7 copy.83
  201.4 1.6 copy-done.4
  203.0 4.8 %fusion.13 = f32[1,32,32,3,3,128]{5,2,4,3,1,0:T(8,128)S(1)} fusion(bf16[3,3,1024,128]{3,2,1,0:T(8,128)(2,1)S(1)} %copy-done.4, bf16[1,32,32,1024]{3,2,1,0:T(8,128)(2,1)} %all-gather.9.cloned.1.call-done), kind=kOutput, calls=%fused_computation.14 | convolution fusion | flops 2415919104 | bytes 9175040 | tf_op jit(solution)/shard_map/bhwc,pqcd->bhwpqd/dot_general | solution.py:14
  207.8 0.7 slice_bitcast_fusion
  208.5 1.3 fusion.39
  209.8 25.0 %reduce-scatter.6.cloned.1.call-done = bf16[3,3,256,128]{2,3,1,0:T(8,128)(2,1)} async-done(((bf16[3,3,1024,128]{2,3,1,0:T(8,128)(2,1)}), bf16[3,3,256,128]{2,3,1,0:T(8,128)(2,1)}) %reduce-scatter.6.cloned.1.call-update) | async-done | bytes 589840 | tf_op jit(solution)/shard_map/reduce_scatter | solution.py:62
  234.8 2.3 copy.45
  237.1 38.2 %reduce-scatter.8.cloned.1.call-done = bf16[3,3,256,128]{2,3,1,0:T(8,128)(2,1)} async-done(((bf16[3,3,1024,128]{2,3,1,0:T(8,128)(2,1)}), bf16[3,3,256,128]{2,3,1,0:T(8,128)(2,1)}) %reduce-scatter.8.cloned.1.call-update) | async-done | bytes 589840 | tf_op jit(solution)/shard_map/reduce_scatter | solution.py:50
  275.3 2.3 copy.46
  (20 shorter events, 0.3 us)
Async XLA Ops:
  7.2 4.3 %copy-start = (bf16[1,32,32,128]{3,2,1,0:T(8,128)(2,1)S(1)}, bf16[1,32,32,128]{3,2,1,0:T(8,128)(2,1)}, u32[]{:S(2)}) copy-start(bf16[1,32,32,128]{3,2,1,0:T(8,128)(2,1)} %param.7) | copy-start | bytes 786436
  7.2 42.9 %all-gather.11.cloned.1.call-start = ((), (), s32[]{:S(2)}) async-start(), calls=%async_computation.6 | async-start | bytes 2949120 | tf_op jit(solution)/shard_map/all_gather | solution.py:48
  7.9 81.5 %all-gather.7.cloned.1.call-start = ((), (), s32[]{:S(2)}) async-start(), calls=%async_computation.4 | async-start | bytes 2949120 | tf_op jit(solution)/shard_map/all_gather | solution.py:43
  8.7 113.2 %all-gather.5.cloned.1.call-start = ((), (), s32[]{:S(2)}) async-start(), calls=%async_computation.3 | async-start | bytes 2359296 | tf_op jit(solution)/shard_map/all_gather | solution.py:44
  9.4 149.5 %reduce-scatter.10.cloned.1.call-start = ((), (), s32[]{:S(2)}) async-start(), calls=%async_computation.9 | async-start | bytes 2359296
  12.1 38.0 %copy-start.2 = (bf16[1,32,32,9,128]{4,2,1,3,0:T(8,128)(2,1)}, bf16[1,32,32,9,128]{4,2,1,3,0:T(8,128)(2,1)S(1)}, u32[]{:S(2)}) copy-start(bf16[1,32,32,9,128]{4,2,1,3,0:T(8,128)(2,1)S(1)} %fusion.55) | copy-start | bytes 7077892
  80.0 115.4 %all-gather.9.cloned.1.call-start = ((), (), s32[]{:S(2)}) async-start(), calls=%async_computation.5 | async-start | bytes 2359296 | tf_op jit(solution)/shard_map/all_gather | solution.py:47
  127.1 2.1 copy-start.1
  165.7 69.1 %reduce-scatter.6.cloned.1.call-start = ((), (), s32[]{:S(2)}) async-start(), calls=%async_computation.7 | async-start | bytes 2949120 | tf_op jit(solution)/shard_map/reduce_scatter | solution.py:62
  165.9 1.6 copy-start.5
  171.5 23.9 %copy-start.3 = (bf16[1,32,32,9,128]{4,2,1,3,0:T(8,128)(2,1)S(1)}, bf16[1,32,32,9,128]{4,2,1,3,0:T(8,128)(2,1)}, u32[]{:S(2)}) copy-start(bf16[1,32,32,9,128]{4,2,1,3,0:T(8,128)(2,1)} %copy-done.2) | copy-start | bytes 7077892
  171.5 103.8 %reduce-scatter.8.cloned.1.call-start = ((), (), s32[]{:S(2)}) async-start(), calls=%async_computation.8 | async-start | bytes 2949120 | tf_op jit(solution)/shard_map/reduce_scatter | solution.py:50
  201.3 1.7 copy-start.4
Sparse Core Ops, SparseCore 0:
  9.9 40.1 all-gather.10
  51.9 37.4 all-gather.6
  91.0 30.8 all-gather.4
  124.0 34.8 reduce-scatter.9
  165.8 29.5 all-gather.8
  198.3 36.4 reduce-scatter.5
  237.9 37.3 reduce-scatter.7
where the time goes:
time: 285 us; the launch traced here: 284 us
  waiting for transfers between devices  197 us (69%)
  local copies, waits for them, and re-layouts  44.9 us (16%)
  matrix products  23.5 us (8%)
  between operations  14.3 us (5%)
  other arithmetic  4.4 us (2%)
    unnamed x34, local copies, waits for them, and re-layouts  40.6 us
    reduce_scatter x1, waiting for transfers between devices, body(): lax.psum_scatter(filter_grads(hidden_all, cotangent).astype(jnp.bfloat16)...  38.2 us
    all_gather x1, waiting for transfers between devices, body(): full_two = lax.all_gather(weight_two, 'dp', axis=2, tiled=True)  38 us
    all_gather x1, waiting for transfers between devices, body(): gathered = lax.all_gather(fields, 'filter', axis=3, tiled=True)  32.5 us
    unnamed x8, waiting for transfers between devices  30.1 us
    reduce_scatter x1, waiting for transfers between devices, body(): lax.psum_scatter(filter_grads(gathered, back_pre).astype(jnp.bfloat16), '...  25 us
    all_gather x1, waiting for transfers between devices, body(): hidden_all = lax.all_gather(hidden, 'filter', axis=3, tiled=True)  23.8 us
    dot_general x2, matrix products, conv_taps(): jnp.einsum('bhwc,pqcd->bhwpqd', inputs, weights, preferred_element_type=j...  9.99 us
  transfers between devices with their start and end apart: 7, of which 7 were waited for; matrix products, arithmetic and copies ran while one was open for 21% of the time, Pallas kernels for 0%

commit v1 on v0

--- a/solution.py
+++ b/solution.py
@@ -40,11 +40,25 @@
 
 
 def body(fields, weight_one, weight_two, cotangent):
+
+    def watch_point_here(local_array):
+        fan = lax.axis_size("filter")
+        store = [(at, (at + 1) % fan) for at in range(fan)]
+        shelf = [(at, (at - 1) % fan) for at in range(fan)]
+        d_next, y_new = ([local_array], [local_array])
+        for _ in range(fan // 2):
+            d_next.append(lax.ppermute(d_next[-1], "filter", store))
+        for _ in range((fan - 1) // 2):
+            y_new.append(lax.ppermute(y_new[-1], "filter", shelf))
+        value_now = jnp.concatenate([*d_next[::-1], *y_new[1:]], 3)
+        b_now = jnp.roll(value_now, (lax.axis_index("filter") - fan // 2) * local_array.shape[3], 3)
+        return b_now
+
     full_one = lax.all_gather(weight_one, "dp", axis=2, tiled=True)
     gathered = lax.all_gather(fields, "filter", axis=3, tiled=True)
     pre_one = conv_taps(gathered, full_one)
     hidden = jax.nn.silu(pre_one).astype(jnp.bfloat16)
-    hidden_all = lax.all_gather(hidden, "filter", axis=3, tiled=True)
+    hidden_all = watch_point_here(hidden)
     full_two = lax.all_gather(weight_two, "dp", axis=2, tiled=True)
     output = conv_taps(hidden_all, full_two).astype(jnp.bfloat16)
     grad_two = lax.psum_scatter(

time: 285 us -> 256 us (0.90)
  waiting for transfers between devices: 197 us -> 158 us
  starting transfers between devices: 0.46 us -> 11.3 us
    reduce_scatter x1, waiting for transfers between devices: 25 us -> 0.01 us  [body(): lax.psum_scatter(filter_grads(gathered, back_pre).astype(jnp.bfloat16), '...]
    all_gather x1 -> x0, waiting for transfers between devices: 23.8 us -> none  [body(): hidden_all = lax.all_gather(hidden, 'filter', axis=3, tiled=True)]
    ppermute x0 -> x7, waiting for transfers between devices: none -> 20.1 us  [the longest x4 20.1 us: watch_point_here(): d_next.append(lax.ppermute(d_next[-1], 'filter', store))]
    ppermute x0 -> x7, starting transfers between devices: none -> 10.9 us  [the longest x3 10.8 us: watch_point_here(): y_new.append(lax.ppermute(y_new[-1], 'filter', shelf))]
    reduce_scatter x1, waiting for transfers between devices: 38.2 us -> 27.8 us  [body(): lax.psum_scatter(filter_grads(hidden_all, cotangent).astype(jnp.bfloat16)...]
    unnamed x34 -> x49, local copies, waits for them, and re-layouts: 40.6 us -> 41.8 us
    unnamed x8 -> x7, waiting for transfers between devices: 30.1 us -> 30.1 us
  transfers between devices with their start and end apart: 7 -> 13, of which waited for: 7 -> 9; matrix products, arithmetic and copies ran while one was open for 21% -> 21% of each run, Pallas kernels for 0% -> 0%
where the time goes in v1:
time: 256 us; the launch traced here: 255 us
  waiting for transfers between devices  158 us (62%)
  local copies, waits for them, and re-layouts  46.4 us (18%)
  matrix products  21.7 us (8%)
  between operations  14.4 us (6%)
  starting transfers between devices  11.3 us (4%)
  other arithmetic  4 us (2%)
    unnamed x49, local copies, waits for them, and re-layouts  41.8 us
    all_gather x1, waiting for transfers between devices, body(): full_two = lax.all_gather(weight_two, 'dp', axis=2, tiled=True)  38 us
    all_gather x1, waiting for transfers between devices, body(): gathered = lax.all_gather(fields, 'filter', axis=3, tiled=True)  32.5 us
    unnamed x7, waiting for transfers between devices  30.1 us
    reduce_scatter x1, waiting for transfers between devices, body(): lax.psum_scatter(filter_grads(hidden_all, cotangent).astype(jnp.bfloat16)...  27.8 us
    ppermute x4, waiting for transfers between devices, watch_point_here(): d_next.append(lax.ppermute(d_next[-1], 'filter', store))  20.1 us
    ppermute x3, starting transfers between devices, watch_point_here(): y_new.append(lax.ppermute(y_new[-1], 'filter', shelf))  10.8 us
    dot_general x2, matrix products, conv_taps(): jnp.einsum('bhwc,pqcd->bhwpqd', inputs, weights, preferred_element_type=j...  9.62 us
  transfers between devices with their start and end apart: 13, of which 9 were waited for; matrix products, arithmetic and copies ran while one was open for 21% of the time, Pallas kernels for 0%

profile of v1, /device:TPU:0, one launch (start us, length us, event | category | flops | bytes accessed | tf_op | source)
XLA Modules:
  0.0 255.4 jit_solution(13173618186684454433)
XLA Ops:
  7.2 0.7 all-gather.8.cloned.1.call-update
  8.0 0.7 all-gather.6.cloned.1.call-update
  8.7 0.7 all-gather.4.cloned.1.call-update
  9.4 1.0 fusion.43
  10.5 1.0 fusion.45
  11.5 0.1 fusion.47
  11.7 0.1 fusion.51
  12.0 0.1 fusion.57
  12.1 38.0 %all-gather.8.cloned.1.call-done = bf16[3,3,1024,128]{3,2,1,0:T(8,128)(2,1)} async-done(((bf16[3,3,256,128]{3,2,1,0:T(8,128)(2,1)}), bf16[3,3,1024,128]{3,2,1,0:T(8,128)(2,1)}) %all-gather.8.cloned.1.call-update) | async-done | bytes 2359312 | tf_op jit(solution)/shard_map/all_gather | solution.py:62
  50.1 5.3 %fusion.16 = bf16[1,32,32,1024]{3,2,1,0:T(8,128)(2,1)S(1)} fusion(bf16[32,32,3,3,128]{4,1,0,3,2:T(8,128)(2,1)} %bitcast.223, bf16[3,3,1024,128]{3,2,1,0:T(8,128)(2,1)} %all-gather.8.cloned.1.call-done), kind=kOutput, calls=%fused_computation.15 | convolution fusion | flops 2416967680 | bytes 6815744 | tf_op jit(solution)/shard_map/bhwpqd,pqcd->bhwc/dot_general | solution.py:34
  55.4 12.2 %copy.60 = bf16[1,32,32,1024]{2,1,0,3:T(8,128)(2,1)} copy(bf16[1,32,32,1024]{3,2,1,0:T(8,128)(2,1)S(1)} %fusion.16) | data formatting | bytes 4194304
  67.5 12.4 %reshape.42 = bf16[1024,1024]{1,0:T(8,128)(2,1)} reshape(bf16[1024,1,32,32]{3,2,1,0:T(8,128)(2,1)} %bitcast.220) | data formatting | bytes 4194304
  80.0 0.2 reduce-scatter.6.cloned.1.call-start
  80.2 9.2 %all-gather.6.cloned.1.call-done = bf16[3,3,1024,128]{3,2,1,0:T(8,128)(2,1)} async-done(((bf16[3,3,256,128]{3,2,1,0:T(8,128)(2,1)}), bf16[3,3,1024,128]{3,2,1,0:T(8,128)(2,1)}) %all-gather.6.cloned.1.call-update) | async-done | bytes 2359312 | tf_op jit(solution)/shard_map/all_gather | solution.py:57
  89.4 32.5 %all-gather.4.cloned.1.call-done = bf16[1,32,32,1024]{3,2,1,0:T(8,128)(2,1)} async-done(((bf16[1,32,32,128]{3,2,1,0:T(8,128)(2,1)}), bf16[1,32,32,1024]{3,2,1,0:T(8,128)(2,1)}) %all-gather.4.cloned.1.call-update) | async-done | bytes 2097168 | tf_op jit(solution)/shard_map/all_gather | solution.py:58
  121.9 5.2 %fusion.10 = f32[1,32,32,3,3,128]{5,2,4,3,1,0:T(8,128)S(1)} fusion(bf16[3,3,1024,128]{3,2,1,0:T(8,128)(2,1)} %all-gather.6.cloned.1.call-done, bf16[1,32,32,1024]{3,2,1,0:T(8,128)(2,1)} %all-gather.4.cloned.1.call-done), kind=kOutput, calls=%fused_computation.13 | convolution fusion | flops 2415919104 | bytes 9175040 | tf_op jit(solution)/shard_map/bhwc,pqcd->bhwpqd/dot_general | solution.py:14
  127.1 2.1 copy-done.1
  129.2 1.7 slice_bitcast_fusion.17
  130.9 28.0 %reduce-scatter.10.cloned.1.call-done = bf16[128,1024]{1,0:T(8,128)(2,1)} async-done(((bf16[1024,1024]{1,0:T(8,128)(2,1)}), bf16[128,1024]{1,0:T(8,128)(2,1)}) %reduce-scatter.10.cloned.1.call-update) | async-done | bytes 262160
  158.9 1.8 reshape.43
  160.7 1.1 copy.61
  161.8 2.2 multiply_convert_fusion
  164.2 0.1 fusion.63
  164.3 0.1 fusion.65
  164.4 0.1 fusion.67
  164.7 0.1 fusion.73
  164.8 0.9 copy-done.6
  165.6 4.0 %fusion = bf16[3,3,1024,128]{2,3,1,0:T(8,128)(2,1)} fusion(bf16[32,32,3,3,128]{4,1,0,3,2:T(8,128)(2,1)S(1)} %bitcast.225, bf16[1,32,32,1024]{3,2,1,0:T(8,128)(2,1)S(1)} %copy-done.6), kind=kOutput, calls=%fused_computation.3 | convolution fusion | flops 2417098752 | bytes 6815744 | tf_op jit(solution)/shard_map/bhwc,bhwpqd->pqcd/dot_general | solution.py:39
  169.7 0.1 multiply_convert_fusion.1
  169.9 7.8 %collective-permute-done = bf16[1,32,32,128]{3,2,1,0:T(8,128)(2,1)S(1)} collective-permute-done((bf16[1,32,32,128]{3,2,1,0:T(8,128)(2,1)S(1)}, bf16[1,32,32,128]{3,2,1,0:T(8,128)(2,1)S(1)}, u32[]{:S(2)}, u32[]{:S(2)}) %collective-permute-start) | collective-permute-done | bytes 262176 | tf_op jit(solution)/shard_map/ppermute | solution.py:50
  177.7 3.5 %collective-permute-start.4 = (bf16[1,32,32,128]{3,2,1,0:T(8,128)(2,1)S(1)}, bf16[1,32,32,128]{3,2,1,0:T(8,128)(2,1)S(1)}, u32[]{:S(2)}, u32[]{:S(2)}) collective-permute-start(bf16[1,32,32,128]{3,2,1,0:T(8,128)(2,1)S(1)} %multiply_convert_fusion.1), channel_id=1, source_target_pairs={{0,7},{1,0},{2,1},{3,2},{4,3},{5,4},{6,5},{7,6},{8,15},{9,8},{10,9... | collective-permute-start | bytes 786440 | tf_op jit(solution)/shard_map/ppermute | solution.py:52
  181.2 4.2 %collective-permute-done.1 = bf16[1,32,32,128]{3,2,1,0:T(8,128)(2,1)S(1)} collective-permute-done((bf16[1,32,32,128]{3,2,1,0:T(8,128)(2,1)S(1)}, bf16[1,32,32,128]{3,2,1,0:T(8,128)(2,1)S(1)}, u32[]{:S(2)}, u32[]{:S(2)}) %collective-permute-start.1) | collective-permute-done | bytes 262176 | tf_op jit(solution)/shard_map/ppermute | solution.py:50
  185.5 3.7 %collective-permute-start.5 = (bf16[1,32,32,128]{3,2,1,0:T(8,128)(2,1)S(1)}, bf16[1,32,32,128]{3,2,1,0:T(8,128)(2,1)S(1)}, u32[]{:S(2)}, u32[]{:S(2)}) collective-permute-start(bf16[1,32,32,128]{3,2,1,0:T(8,128)(2,1)S(1)} %collective-permute-done.4), channel_id=1, source_target_pairs={{0,7},{1,0},{2,1},{3,2},{4,3},{5,4},{6,5},{7,6},{8,15},{9,8},{10,9... | collective-permute-start | bytes 786440 | tf_op jit(solution)/shard_map/ppermute | solution.py:52
  189.2 4.0 %collective-permute-done.2 = bf16[1,32,32,128]{3,2,1,0:T(8,128)(2,1)S(1)} collective-permute-done((bf16[1,32,32,128]{3,2,1,0:T(8,128)(2,1)S(1)}, bf16[1,32,32,128]{3,2,1,0:T(8,128)(2,1)S(1)}, u32[]{:S(2)}, u32[]{:S(2)}) %collective-permute-start.2) | collective-permute-done | bytes 262176 | tf_op jit(solution)/shard_map/ppermute | solution.py:50
  193.2 3.5 %collective-permute-start.6 = (bf16[1,32,32,128]{3,2,1,0:T(8,128)(2,1)S(1)}, bf16[1,32,32,128]{3,2,1,0:T(8,128)(2,1)S(1)}, u32[]{:S(2)}, u32[]{:S(2)}) collective-permute-start(bf16[1,32,32,128]{3,2,1,0:T(8,128)(2,1)S(1)} %collective-permute-done.5), channel_id=1, source_target_pairs={{0,7},{1,0},{2,1},{3,2},{4,3},{5,4},{6,5},{7,6},{8,15},{9,8},{10,9... | collective-permute-start | bytes 786440 | tf_op jit(solution)/shard_map/ppermute | solution.py:52
  196.8 4.0 %collective-permute-done.3 = bf16[1,32,32,128]{3,2,1,0:T(8,128)(2,1)S(1)} collective-permute-done((bf16[1,32,32,128]{3,2,1,0:T(8,128)(2,1)S(1)}, bf16[1,32,32,128]{3,2,1,0:T(8,128)(2,1)S(1)}, u32[]{:S(2)}, u32[]{:S(2)}) %collective-permute-start.3) | collective-permute-done | bytes 262176 | tf_op jit(solution)/shard_map/ppermute | solution.py:50
  201.2 0.2 constant_dynamic-update-slice_fusion.11
  202.0 0.2 constant_dynamic-update-slice_fusion.3
  202.5 0.8 copy-done.3
  203.3 2.9 %fusion.4 = bf16[3,3,128,1024,1]{3,2,0,1,4:T(8,128)(2,1)S(1)} fusion(bf16[32,32,3,3,128]{4,1,0,3,2:T(8,128)(2,1)S(1)} %bitcast.224, bf16[1,32,32,2048]{3,2,1,0:T(8,128)(2,1)S(1)} %constant_dynamic-update-slice_fusion, s32[]{:T(128)S(6)} %select_n.14), kind=kOutput, calls=%fused_computation.7 | convolution fusion | flops 2415919104 | bytes 6815748 | tf_op jit(solution)/shard_map/bhwc,bhwpqd->pqcd/dot_general | solution.py:39
  206.2 1.8 copy.83
  208.1 1.6 copy-done.5
  209.7 4.5 %fusion.13 = f32[1,32,32,3,3,128]{5,2,4,3,1,0:T(8,128)S(1)} fusion(bf16[3,3,1024,128]{3,2,1,0:T(8,128)(2,1)S(1)} %copy-done.5, bf16[1,32,32,2048]{3,2,1,0:T(8,128)(2,1)} %copy-done.4, s32[]{:T(128)S(6)} %select_n.14), kind=kOutput, calls=%fused_computation.14 | convolution fusion | flops 2415919104 | bytes 9175044 | tf_op jit(solution)/shard_map/bhwc,pqcd->bhwpqd/dot_general | solution.py:14
  214.2 0.7 slice_bitcast_fusion
  214.9 1.3 fusion.41
  216.2 2.3 copy.45
  218.5 27.8 %reduce-scatter.8.cloned.1.call-done = bf16[3,3,256,128]{2,3,1,0:T(8,128)(2,1)} async-done(((bf16[3,3,1024,128]{2,3,1,0:T(8,128)(2,1)}), bf16[3,3,256,128]{2,3,1,0:T(8,128)(2,1)}) %reduce-scatter.8.cloned.1.call-update) | async-done | bytes 589840 | tf_op jit(solution)/shard_map/reduce_scatter | solution.py:64
  246.2 2.3 copy.46
  (49 shorter events, 2.1 us)
Async XLA Ops:
  7.2 4.3 %copy-start = (bf16[1,32,32,128]{3,2,1,0:T(8,128)(2,1)S(1)}, bf16[1,32,32,128]{3,2,1,0:T(8,128)(2,1)}, u32[]{:S(2)}) copy-start(bf16[1,32,32,128]{3,2,1,0:T(8,128)(2,1)} %param.7) | copy-start | bytes 786436
  7.2 42.9 %all-gather.8.cloned.1.call-start = ((), (), s32[]{:S(2)}) async-start(), calls=%async_computation.5 | async-start | bytes 2949120 | tf_op jit(solution)/shard_map/all_gather | solution.py:62
  7.9 81.5 %all-gather.6.cloned.1.call-start = ((), (), s32[]{:S(2)}) async-start(), calls=%async_computation.4 | async-start | bytes 2949120 | tf_op jit(solution)/shard_map/all_gather | solution.py:57
  8.7 113.2 %all-gather.4.cloned.1.call-start = ((), (), s32[]{:S(2)}) async-start(), calls=%async_computation.3 | async-start | bytes 2359296 | tf_op jit(solution)/shard_map/all_gather | solution.py:58
  9.4 149.5 %reduce-scatter.10.cloned.1.call-start = ((), (), s32[]{:S(2)}) async-start(), calls=%async_computation.8 | async-start | bytes 2359296
  12.1 38.0 %copy-start.2 = (bf16[1,32,32,9,128]{4,2,1,3,0:T(8,128)(2,1)}, bf16[1,32,32,9,128]{4,2,1,3,0:T(8,128)(2,1)S(1)}, u32[]{:S(2)}) copy-start(bf16[1,32,32,9,128]{4,2,1,3,0:T(8,128)(2,1)S(1)} %fusion.57) | copy-start | bytes 7077892
  80.0 136.2 %reduce-scatter.6.cloned.1.call-start = ((), (), s32[]{:S(2)}) async-start(), calls=%async_computation.6 | async-start | bytes 2949120 | tf_op jit(solution)/shard_map/reduce_scatter | solution.py:76
  127.1 2.1 copy-start.1
  164.0 1.6 copy-start.6
  169.7 76.6 %reduce-scatter.8.cloned.1.call-start = ((), (), s32[]{:S(2)}) async-start(), calls=%async_computation.7 | async-start | bytes 2949120 | tf_op jit(solution)/shard_map/reduce_scatter | solution.py:64
  169.9 7.8 %collective-permute-start = (bf16[1,32,32,128]{3,2,1,0:T(8,128)(2,1)S(1)}, bf16[1,32,32,128]{3,2,1,0:T(8,128)(2,1)S(1)}, u32[]{:S(2)}, u32[]{:S(2)}) collective-permute-start(bf16[1,32,32,128]{3,2,1,0:T(8,128)(2,1)S(1)} %multiply_convert_fusion.1), channel_id=1, source_target_pairs={{0,1},{1,2},{2,3},{3,4},{4,5},{5,6},{6,7},{7,0},{8,9},{9,10},{10,1... | collective-permute-start | bytes 786440 | tf_op jit(solution)/shard_map/ppermute | solution.py:50
  177.7 7.8 %collective-permute-start.1 = (bf16[1,32,32,128]{3,2,1,0:T(8,128)(2,1)S(1)}, bf16[1,32,32,128]{3,2,1,0:T(8,128)(2,1)S(1)}, u32[]{:S(2)}, u32[]{:S(2)}) collective-permute-start(bf16[1,32,32,128]{3,2,1,0:T(8,128)(2,1)S(1)} %collective-permute-done), channel_id=1, source_target_pairs={{0,1},{1,2},{2,3},{3,4},{4,5},{5,6},{6,7},{7,0},{8,9},{9,10},{10,1... | collective-permute-start | bytes 786440 | tf_op jit(solution)/shard_map/ppermute | solution.py:50
  177.7 7.8 %collective-permute-start.4 = (bf16[1,32,32,128]{3,2,1,0:T(8,128)(2,1)S(1)}, bf16[1,32,32,128]{3,2,1,0:T(8,128)(2,1)S(1)}, u32[]{:S(2)}, u32[]{:S(2)}) collective-permute-start(bf16[1,32,32,128]{3,2,1,0:T(8,128)(2,1)S(1)} %multiply_convert_fusion.1), channel_id=1, source_target_pairs={{0,7},{1,0},{2,1},{3,2},{4,3},{5,4},{6,5},{7,6},{8,15},{9,8},{10,9... | collective-permute-start | bytes 786440 | tf_op jit(solution)/shard_map/ppermute | solution.py:52
  185.5 7.8 %collective-permute-start.2 = (bf16[1,32,32,128]{3,2,1,0:T(8,128)(2,1)S(1)}, bf16[1,32,32,128]{3,2,1,0:T(8,128)(2,1)S(1)}, u32[]{:S(2)}, u32[]{:S(2)}) collective-permute-start(bf16[1,32,32,128]{3,2,1,0:T(8,128)(2,1)S(1)} %collective-permute-done.1), channel_id=1, source_target_pairs={{0,1},{1,2},{2,3},{3,4},{4,5},{5,6},{6,7},{7,0},{8,9},{9,10},{10,1... | collective-permute-start | bytes 786440 | tf_op jit(solution)/shard_map/ppermute | solution.py:50
  185.5 7.8 %collective-permute-start.5 = (bf16[1,32,32,128]{3,2,1,0:T(8,128)(2,1)S(1)}, bf16[1,32,32,128]{3,2,1,0:T(8,128)(2,1)S(1)}, u32[]{:S(2)}, u32[]{:S(2)}) collective-permute-start(bf16[1,32,32,128]{3,2,1,0:T(8,128)(2,1)S(1)} %collective-permute-done.4), channel_id=1, source_target_pairs={{0,7},{1,0},{2,1},{3,2},{4,3},{5,4},{6,5},{7,6},{8,15},{9,8},{10,9... | collective-permute-start | bytes 786440 | tf_op jit(solution)/shard_map/ppermute | solution.py:52
  193.2 7.6 %collective-permute-start.3 = (bf16[1,32,32,128]{3,2,1,0:T(8,128)(2,1)S(1)}, bf16[1,32,32,128]{3,2,1,0:T(8,128)(2,1)S(1)}, u32[]{:S(2)}, u32[]{:S(2)}) collective-permute-start(bf16[1,32,32,128]{3,2,1,0:T(8,128)(2,1)S(1)} %collective-permute-done.2), channel_id=1, source_target_pairs={{0,1},{1,2},{2,3},{3,4},{4,5},{5,6},{6,7},{7,0},{8,9},{9,10},{10,1... | collective-permute-start | bytes 786440 | tf_op jit(solution)/shard_map/ppermute | solution.py:50
  193.2 8.3 %collective-permute-start.6 = (bf16[1,32,32,128]{3,2,1,0:T(8,128)(2,1)S(1)}, bf16[1,32,32,128]{3,2,1,0:T(8,128)(2,1)S(1)}, u32[]{:S(2)}, u32[]{:S(2)}) collective-permute-start(bf16[1,32,32,128]{3,2,1,0:T(8,128)(2,1)S(1)} %collective-permute-done.5), channel_id=1, source_target_pairs={{0,7},{1,0},{2,1},{3,2},{4,3},{5,4},{6,5},{7,6},{8,15},{9,8},{10,9... | collective-permute-start | bytes 786440 | tf_op jit(solution)/shard_map/ppermute | solution.py:52
  201.6 1.7 copy-start.3
  203.3 2.9 %copy-start.4 = (bf16[1,32,32,2048]{3,2,1,0:T(8,128)(2,1)}, bf16[1,32,32,2048]{3,2,1,0:T(8,128)(2,1)S(1)}, u32[]{:S(2)}) copy-start(bf16[1,32,32,2048]{3,2,1,0:T(8,128)(2,1)S(1)} %constant_dynamic-update-slice_fusion) | copy-start | bytes 12582916
  208.0 1.7 copy-start.5
Sparse Core Ops, SparseCore 0:
  9.9 40.1 all-gather.7
  51.9 37.4 all-gather.5
  91.0 30.8 all-gather.3
  124.0 34.8 reduce-scatter.9
  169.8 36.0 reduce-scatter.5
  208.8 37.3 reduce-scatter.7
